TPU v7x, 512 devices: a whole 4x8x8 slice. The times are simulated.
512 devices in a mesh: prompt: 16 (over x, y_lo), feat: 32 (over y_hi, z, core).
Axes of the slice: x: 4, y: 8 (y_hi: 2, y_lo: 4; y = y_hi * 4 + y_lo), z: 8, core: 2. Of those that a mesh axis runs over, the one named last changes fastest.
Arguments:
- decoder: bfloat16 [8192, 5376], P('feat'), may hold values from -0.078125 to 0.078125
- encoder: bfloat16 [24576, 5376], P(('feat', 'prompt')), may hold values from -6 to 6
- row_ids: int32 [16, 512], P('prompt', 'feat'), may hold values from 0 to 255
- counts: int32 [16, 32], P('prompt'), may hold values from 1 to 16, 307 in all within a row
- activity: float32 [16, 512], P('prompt'), may hold values from 0.25 to 4
Outputs:
- edges: bfloat16 [16, 512, 24576], P('prompt', None, 'feat')
Inputs may be any that keep to these rules, and one draw needn't show every extreme that they name: counts of one prompt sum to 307; some owner of each prompt holds exactly 16.
All inputs are finite; a program needn't handle non-finite values.
Results may differ from a plain program's by a relative error of at most 0.001.
Values may be sent and summed in bfloat16 or wider, within the bound.
No kernel may reach another device: no remote copies, remote signals or barrier semaphores. Data moves between devices by JAX's collectives and lax.ppermute only.
A program may use at most 64 MiB of HBM per device.

v0:
```python
import jax
import jax.numpy as jnp
from jax import lax
from jax.sharding import PartitionSpec as P


def per_device(decoder, encoder, row_ids, counts, activity):
    slot_count = row_ids.shape[1]
    owner_index = lax.axis_index("feat")
    picked_rows = jnp.take(decoder, row_ids[0], axis=0)
    live_count = lax.dynamic_index_in_dim(counts[0], owner_index, 0, keepdims=False)
    live_slots = jnp.arange(slot_count, dtype=jnp.int32) < live_count
    source_rows = jnp.where(live_slots[:, None], picked_rows, jnp.zeros((), picked_rows.dtype))
    weights = activity[0]
    whole_rows = lax.all_gather(source_rows, "feat", axis=0, tiled=True)
    products = lax.dot_general(
        whole_rows,
        lax.all_gather(encoder, "prompt", axis=0, tiled=True),
        (((1,), (1,)), ((), ())),
        preferred_element_type=jnp.float32,
    )
    edges = (weights[:, None] * products).astype(jnp.bfloat16)
    return edges[None]


def solution(mesh):
    in_specs = (
        P("feat", None),
        P(("feat", "prompt"), None),
        P("prompt", "feat"),
        P("prompt", None),
        P("prompt", None),
    )
    out_specs = P("prompt", None, "feat")
    return jax.shard_map(
        per_device, mesh=mesh, in_specs=in_specs, out_specs=out_specs, check_vma=False
    )
```

profile of v0, /device:TPU:1, one launch (start us, length us, event | category | flops | bytes accessed | tf_op | source)
XLA Modules:
  0.0 330.1 jit_solution(3956088950940566915)
XLA Ops:
  6.5 0.0 copy-start
  6.5 0.0 all-gather.3.cloned.1.call-start
  6.5 0.8 fusion.1
  7.3 1.3 constant_dynamic-slice_fusion
  8.6 1.3 compare_and_fusion
  9.9 0.0 copy-done
  9.9 0.7 gather_fusion
  10.6 0.8 select_select_fusion
  11.4 0.0 all-gather.3.cloned.1.call-update
  11.4 0.0 all-gather.5.cloned.1.call-start
  11.4 0.7 all-gather.5.cloned.1.call-update
  12.1 120.5 %all-gather.3.cloned.1.call-done = bf16[512,5376]{1,0:T(8,128)(2,1)} async-done(((bf16[16,5376]{1,0:T(8,128)(2,1)}), bf16[512,5376]{1,0:T(8,128)(2,1)}) %all-gather.3.cloned.1.call-update) | async-done | bytes 5505040 | tf_op jit(solution)/shard_map/all_gather | solution.py:15
  132.7 180.4 %all-gather.5.cloned.1.call-done = bf16[768,5376]{1,0:T(8,128)(2,1)} async-done(((bf16[48,5376]{1,0:T(8,128)(2,1)}), bf16[768,5376]{1,0:T(8,128)(2,1)}) %all-gather.5.cloned.1.call-update) | async-done | bytes 8257552 | tf_op jit(solution)/shard_map/all_gather | solution.py:18
  313.0 10.2 %fusion = bf16[1,512,768]{2,1,0:T(8,128)(2,1)} fusion(bf16[512,5376]{1,0:T(8,128)(2,1)} %all-gather.3.cloned.1.call-done, bf16[768,5376]{1,0:T(8,128)(2,1)} %all-gather.5.cloned.1.call-done, f32[512]{0:T(512)} %bitcast.12), kind=kOutput, calls=%fused_computation.2 | convolution fusion | flops 4228644864 | bytes 14551040 | tf_op jit(solution)/shard_map/dot_general | solution.py:16
  (1 shorter events, 0.0 us)
Async XLA Ops:
  6.5 3.4 %copy-start = (bf16[256,5376]{1,0:T(8,128)(2,1)S(1)}, bf16[256,5376]{1,0:T(8,128)(2,1)}, u32[]{:S(2)}) copy-start(bf16[256,5376]{1,0:T(8,128)(2,1)} %param.5) | copy-start | bytes 8257540
  6.5 126.1 %all-gather.3.cloned.1.call-start = ((), (), s32[]{:S(2)}) async-start(), calls=%async_computation | async-start | bytes 5677056 | tf_op jit(solution)/shard_map/all_gather | solution.py:15
  11.4 301.6 %all-gather.5.cloned.1.call-start = ((), (), s32[]{:S(2)}) async-start(), calls=%async_computation.1 | async-start | bytes 8773632 | tf_op jit(solution)/shard_map/all_gather | solution.py:18
Sparse Core Ops, SparseCore 0:
  11.5 121.0 all-gather.2
  134.7 178.2 all-gather.4
where the time goes:
time: 330 us
  waiting for transfers between devices  302 us (92%)
  between operations  13.4 us (4%)
  matrix products  10.2 us (3%)
    all_gather x1, waiting for transfers between devices, per_device(): lax.all_gather(encoder, 'prompt', axis=0, tiled=True)  180 us
    all_gather x1, waiting for transfers between devices, per_device(): whole_rows = lax.all_gather(source_rows, 'feat', axis=0, tiled=True)  121 us
    dot_general x1, matrix products, per_device(): lax.dot_general(whole_rows, lax.all_gather(encoder, 'prompt', axis=0, til...  10.2 us
  transfers between devices with their start and end apart: 2, of which 2 were waited for; matrix products, arithmetic and copies ran while one was open for 0% of the time, Pallas kernels for 0%

commit v1 on v0

--- a/solution.py
+++ b/solution.py
@@ -12,7 +12,9 @@
     live_slots = jnp.arange(slot_count, dtype=jnp.int32) < live_count
     source_rows = jnp.where(live_slots[:, None], picked_rows, jnp.zeros((), picked_rows.dtype))
     weights = activity[0]
-    whole_rows = lax.all_gather(source_rows, "feat", axis=0, tiled=True)
+    whole_rows = jnp.concatenate(
+        lax.all_to_all(jnp.stack([source_rows] * lax.axis_size("feat")), "feat", 0, 0), axis=0
+    )
     products = lax.dot_general(
         whole_rows,
         lax.all_gather(encoder, "prompt", axis=0, tiled=True),

time: 330 us -> 334 us (1.012)
  blocking collectives: 0 us -> 174 us
  waiting for transfers between devices: 302 us -> 132 us
    all_to_all x0 -> x1, blocking collectives: none -> 174 us  [per_device(): lax.all_to_all(jnp.stack([source_rows] * lax.axis_size('feat')), 'feat',...]
    all_gather x1 -> x0, waiting for transfers between devices: 121 us -> none  [per_device(): whole_rows = lax.all_gather(source_rows, 'feat', axis=0, tiled=True)]
    all_gather x1, waiting for transfers between devices: 180 us -> 131 us  [per_device(): lax.all_gather(encoder, 'prompt', axis=0, tiled=True)]
  transfers between devices with their start and end apart: 2 -> 1, of which waited for: 2 -> 1; matrix products, arithmetic and copies ran while one was open for 0% -> 1% of each run, Pallas kernels for 0% -> 0%
where the time goes in v1:
time: 334 us
  blocking collectives  174 us (52%)
  waiting for transfers between devices  132 us (40%)
  between operations  13.4 us (4%)
  matrix products  10.3 us (3%)
    all_to_all x1, blocking collectives, per_device(): lax.all_to_all(jnp.stack([source_rows] * lax.axis_size('feat')), 'feat',...  174 us
    all_gather x1, waiting for transfers between devices, per_device(): lax.all_gather(encoder, 'prompt', axis=0, tiled=True)  131 us
    dot_general x1, matrix products, per_device(): lax.dot_general(whole_rows, lax.all_gather(encoder, 'prompt', axis=0, til...  10.3 us
  transfers between devices with their start and end apart: 1, of which 1 were waited for; matrix products, arithmetic and copies ran while one was open for 1% of the time, Pallas kernels for 0%

profile of v1, /device:TPU:1, one launch (start us, length us, event | category | flops | bytes accessed | tf_op | source)
XLA Modules:
  0.0 334.1 jit_solution(10667212578584669589)
XLA Ops:
  6.5 0.0 copy-start
  6.5 0.0 all-gather.2.cloned.1.call-start
  6.5 0.7 all-gather.2.cloned.1.call-update
  7.3 1.3 constant_dynamic-slice_fusion
  8.6 0.7 fusion.1
  9.3 0.0 copy-done
  9.3 0.7 gather_fusion
  9.9 1.3 compare_and_fusion
  11.2 0.1 select_select_fusion
  11.3 0.4 stack.2
  11.7 0.0 copy-start.1
  11.7 173.9 %all_to_all.5 = bf16[32,16,5376]{2,1,0:T(8,128)(2,1)} all-to-all(bf16[32,16,5376]{2,1,0:T(8,128)(2,1)S(1)} %stack.2), channel_id=1, replica_groups=mesh['prompt'=16,'feat'=32] {'feat'}, dimensions={0} | all-to-all | bytes 11010048 | tf_op jit(solution)/shard_map/all_to_all | solution.py:16
  185.7 131.2 %all-gather.2.cloned.1.call-done = bf16[768,5376]{1,0:T(8,128)(2,1)} async-done(((bf16[48,5376]{1,0:T(8,128)(2,1)}), bf16[768,5376]{1,0:T(8,128)(2,1)}) %all-gather.2.cloned.1.call-update) | async-done | bytes 8257552 | tf_op jit(solution)/shard_map/all_gather | solution.py:20
  316.9 0.0 copy-done.1
  316.9 10.3 %fusion = bf16[1,512,768]{2,1,0:T(8,128)(2,1)} fusion(bf16[512,5376]{1,0:T(8,128)(2,1)} %bitcast.13, bf16[768,5376]{1,0:T(8,128)(2,1)} %all-gather.2.cloned.1.call-done, f32[512]{0:T(512)S(1)} %bitcast.14), kind=kOutput, calls=%fused_computation.2 | convolution fusion | flops 4228644864 | bytes 14551040 | tf_op jit(solution)/shard_map/dot_general | solution.py:18
  (1 shorter events, 0.0 us)
Async XLA Ops:
  6.5 2.7 copy-start
  6.5 310.4 %all-gather.2.cloned.1.call-start = ((), (), s32[]{:S(2)}) async-start(), calls=%async_computation.1 | async-start | bytes 8773632 | tf_op jit(solution)/shard_map/all_gather | solution.py:20
  11.7 305.2 %copy-start.1 = (f32[1,512]{1,0:T(1,128)S(1)}, f32[1,512]{1,0:T(1,128)}, u32[]{:S(2)}) copy-start(f32[1,512]{1,0:T(1,128)} %param.9) | copy-start | bytes 6148
Sparse Core Ops, SparseCore 0:
  9.4 307.4 all-gather.1
